TPU v7x, 32 devices: a whole 2x2x4 slice. The times are simulated.
32 devices in a mesh: group: 2 (over y), replica: 16 (over z, x, core).
Axes of the slice: x: 2, y: 2, z: 4, core: 2. Of those that a mesh axis runs over, the one named last changes fastest.
Arguments:
- tokens: bfloat16 [32, 144, 896], P(('group', 'replica')), may hold values from -6 to 6
- segments: int32 [32, 144], P(('group', 'replica')), may hold values from 0 to 35, never falling along the last dimension, each value on 1 to 72 neighbouring positions
- norm1_gain: bfloat16 [896], P('group'), may hold values from 0.5 to 1.5
- qkv_weight: bfloat16 [896, 1152], P('group'), may hold values from -0.1875 to 0.1875
- qkv_bias: bfloat16 [1152], P('group'), may hold values from -2.5 to 2.5
- out_weight: bfloat16 [896, 896], P('group'), may hold values from -0.375 to 0.375
- norm2_gain: bfloat16 [896], P('group'), may hold values from 0.5 to 1.5
- gate_weight: bfloat16 [896, 4864], P(None, 'group'), may hold values from -0.1875 to 0.1875
- up_weight: bfloat16 [896, 4864], P(None, 'group'), may hold values from -0.1875 to 0.1875
- down_weight: bfloat16 [4864, 896], P('group'), may hold values from -0.078125 to 0.078125
- cotangent: bfloat16 [32, 144, 896], P(('group', 'replica')), may hold values from -6 to 6
Outputs:
- result: float32 [32, 144, 896], P(('group', 'replica'))
- back_tokens: float32 [32, 144, 896], P(('group', 'replica'))
- grad_norm1: float32 [896], P('group')
- grad_qkv: float32 [896, 1152], P('group')
- grad_bias: float32 [1152], P('group')
- grad_out: float32 [896, 896], P('group')
- grad_norm2: float32 [896], P('group')
- grad_gate: float32 [896, 4864], P(None, 'group')
- grad_up: float32 [896, 4864], P(None, 'group')
- grad_down: float32 [4864, 896], P('group')
Inputs may be any that keep to these rules, and one draw needn't show every extreme that they name: `segments`: segment ids never fall along a sequence.
All inputs are finite; a program needn't handle non-finite values.
Results may differ from a plain program's by a relative error of at most 0.023.
Values may be sent and summed in bfloat16 or wider, within the bound.
A program may use at most 192 MiB of HBM per device.

v0:
```python
import jax
import jax.numpy as jnp
from jax import lax
from jax.sharding import PartitionSpec as P

H = 14
KV = 2
HD = 64
EPSILON = 1e-06
ROPE_BASE = 1000000.0
NEG_LARGE = -1e30


def doc_layout(segments, head_dim):
    length = segments.shape[1]
    places = jnp.arange(length, dtype=jnp.int32)
    same_doc = segments[:, :, None] == segments[:, None, :]
    earlier = places[None, None, :] < places[None, :, None]
    positions = jnp.sum(jnp.where(same_doc & earlier, 1.0, 0.0).astype(jnp.float32), axis=2)
    allowed = jnp.where(same_doc & (places[None, None, :] <= places[None, :, None]), 1, 0).astype(
        jnp.int32
    )
    half_dim = head_dim // 2
    frequency = ROPE_BASE ** (-2.0 * jnp.arange(half_dim, dtype=jnp.float32) / head_dim)
    angles = positions[:, :, None] * frequency[None, None, :]
    return (allowed, jnp.cos(angles)[:, :, None, :], jnp.sin(angles)[:, :, None, :])


def rotate(values, cosine, sine):
    half_dim = values.shape[-1] // 2
    front_half = values[..., :half_dim]
    back_half = values[..., half_dim:]
    return jnp.concatenate(
        [front_half * cosine - back_half * sine, back_half * cosine + front_half * sine], axis=-1
    )


def unrotate(gradients, cosine, sine):
    half_dim = gradients.shape[-1] // 2
    front_half = gradients[..., :half_dim]
    back_half = gradients[..., half_dim:]
    return jnp.concatenate(
        [front_half * cosine + back_half * sine, back_half * cosine - front_half * sine], axis=-1
    )


def inverse_rms(hidden):
    return lax.rsqrt(jnp.mean(hidden * hidden, axis=-1, keepdims=True) + EPSILON)


def norm_backward(hidden, inv_rms, gain_f, back_normed):
    weighted = back_normed * gain_f
    inner = jnp.mean(weighted * hidden, axis=-1, keepdims=True)
    back_hidden = inv_rms * weighted - hidden * (inv_rms * inv_rms * inv_rms) * inner
    back_gain = jnp.sum(back_normed * hidden * inv_rms, axis=0)
    return (back_hidden, back_gain)


def matmul(left, right):
    return jnp.dot(left, right, preferred_element_type=jnp.float32)


def outer_sum(left, right):
    return lax.dot_general(
        left, right, (((0,), (0,)), ((), ())), preferred_element_type=jnp.float32
    )


def times_transposed(left, right):
    return lax.dot_general(
        left, right, (((1,), (1,)), ((), ())), preferred_element_type=jnp.float32
    )


def score_block(query_b, keys_b, allowed, score_scale):
    scores = (
        jnp.einsum("sqkgd,spkd->skgqp", query_b, keys_b, preferred_element_type=jnp.float32)
        * score_scale
    )
    return jnp.where(allowed[:, None, None, :, :] > 0, scores, NEG_LARGE)


def on_device(
    tokens,
    segments,
    norm1_gain,
    qkv_weight,
    qkv_bias,
    out_weight,
    norm2_gain,
    gate_weight,
    up_weight,
    down_weight,
    cotangent,
):
    sequences, length, model_width = tokens.shape
    row_count = sequences * length
    q_width = H * HD
    kv_width = KV * HD
    groups = H // KV
    score_scale = HD ** (-0.5)
    gain1_b, w_qkv, b_qkv, w_out, gain2_b = (
        lax.all_gather(norm1_gain, "group", axis=0, tiled=True),
        lax.all_gather(qkv_weight, "group", axis=0, tiled=True),
        lax.all_gather(qkv_bias, "group", axis=0, tiled=True),
        lax.all_gather(out_weight, "group", axis=0, tiled=True),
        lax.all_gather(norm2_gain, "group", axis=0, tiled=True),
    )
    allowed, cosine, sine = doc_layout(segments, HD)
    resid_in = tokens.reshape(row_count, model_width).astype(jnp.float32)
    inv_rms1 = inverse_rms(resid_in)
    gain1 = gain1_b.astype(jnp.float32)
    normed1 = (resid_in * inv_rms1 * gain1).astype(jnp.bfloat16)
    projected = matmul(normed1, w_qkv) + b_qkv.astype(jnp.float32)
    query = projected[:, :q_width].reshape(sequences, length, H, HD)
    keys_raw = projected[:, q_width : q_width + kv_width].reshape(sequences, length, KV, HD)
    values_raw = projected[:, q_width + kv_width :].reshape(sequences, length, KV, HD)
    query_b = (
        rotate(query, cosine, sine).astype(jnp.bfloat16).reshape(sequences, length, KV, groups, HD)
    )
    keys_b = rotate(keys_raw, cosine, sine).astype(jnp.bfloat16)
    values_b = values_raw.astype(jnp.bfloat16)
    scores = score_block(query_b, keys_b, allowed, score_scale)
    top_score = jnp.max(scores, axis=-1, keepdims=True)
    log_total = top_score + jnp.log(jnp.sum(jnp.exp(scores - top_score), axis=-1, keepdims=True))
    soft_b = jnp.exp(scores - log_total).astype(jnp.bfloat16)
    context = jnp.einsum("skgqp,spkd->sqkgd", soft_b, values_b, preferred_element_type=jnp.float32)
    context_b = context.astype(jnp.bfloat16).reshape(row_count, q_width)
    middle = resid_in + matmul(context_b, w_out)
    inv_rms2 = inverse_rms(middle)
    gain2 = gain2_b.astype(jnp.float32)
    normed2 = (middle * inv_rms2 * gain2).astype(jnp.bfloat16)
    back_rows = cotangent.reshape(row_count, model_width)
    normed_all, back_all = (
        lax.all_gather(normed2, "group", axis=0, tiled=True),
        lax.all_gather(back_rows, "group", axis=0, tiled=True),
    )
    gate_pre = matmul(normed_all, gate_weight)
    up_proj = matmul(normed_all, up_weight)
    sigmoid_gate = jax.nn.sigmoid(gate_pre)
    silu_gate = gate_pre * sigmoid_gate
    activ_b = (silu_gate * up_proj).astype(jnp.bfloat16)
    result = middle + lax.psum_scatter(
        matmul(activ_b, down_weight).astype(jnp.bfloat16), "group", scatter_dimension=0, tiled=True
    ).astype(jnp.float32)
    back_activ = times_transposed(back_all, down_weight)
    back_gate = (
        back_activ * up_proj * sigmoid_gate * (1.0 + gate_pre * (1.0 - sigmoid_gate))
    ).astype(jnp.bfloat16)
    back_up = (back_activ * silu_gate).astype(jnp.bfloat16)
    grad_down = outer_sum(activ_b, back_all)
    grad_gate = outer_sum(normed_all, back_gate)
    grad_up = outer_sum(normed_all, back_up)
    local_normed = times_transposed(back_gate, gate_weight) + times_transposed(back_up, up_weight)
    back_normed2 = lax.psum_scatter(
        local_normed.astype(jnp.bfloat16), "group", scatter_dimension=0, tiled=True
    ).astype(jnp.float32)
    gain1_b, w_qkv, b_qkv, w_out, gain2_b = (
        lax.all_gather(norm1_gain, "group", axis=0, tiled=True),
        lax.all_gather(qkv_weight, "group", axis=0, tiled=True),
        lax.all_gather(qkv_bias, "group", axis=0, tiled=True),
        lax.all_gather(out_weight, "group", axis=0, tiled=True),
        lax.all_gather(norm2_gain, "group", axis=0, tiled=True),
    )
    gain1 = gain1_b.astype(jnp.float32)
    gain2 = gain2_b.astype(jnp.float32)
    back_norm2, grad_norm2_part = norm_backward(middle, inv_rms2, gain2, back_normed2)
    back_middle = back_rows.astype(jnp.float32) + back_norm2
    back_middle_b = back_middle.astype(jnp.bfloat16)
    grad_out_part = outer_sum(context_b, back_middle_b)
    back_context = times_transposed(back_middle_b, w_out).astype(jnp.bfloat16)
    back_context = back_context.reshape(sequences, length, KV, groups, HD)
    soft = jnp.exp(score_block(query_b, keys_b, allowed, score_scale) - log_total)
    soft_again = soft.astype(jnp.bfloat16)
    back_values = jnp.einsum(
        "skgqp,sqkgd->spkd", soft_again, back_context, preferred_element_type=jnp.float32
    )
    back_soft = jnp.einsum(
        "sqkgd,spkd->skgqp", back_context, values_b, preferred_element_type=jnp.float32
    )
    row_dot = jnp.sum(soft * back_soft, axis=-1, keepdims=True)
    back_scores = (soft * (back_soft - row_dot) * score_scale).astype(jnp.bfloat16)
    back_query = jnp.einsum(
        "skgqp,spkd->sqkgd", back_scores, keys_b, preferred_element_type=jnp.float32
    )
    back_keys = jnp.einsum(
        "skgqp,sqkgd->spkd", back_scores, query_b, preferred_element_type=jnp.float32
    )
    back_query = unrotate(back_query.reshape(sequences, length, H, HD), cosine, sine)
    back_keys = unrotate(back_keys, cosine, sine)
    back_proj = jnp.concatenate(
        [
            back_query.reshape(row_count, q_width),
            back_keys.reshape(row_count, kv_width),
            back_values.reshape(row_count, kv_width),
        ],
        axis=1,
    )
    grad_bias_part = jnp.sum(back_proj, axis=0)
    back_proj_b = back_proj.astype(jnp.bfloat16)
    grad_qkv_part = outer_sum(normed1, back_proj_b)
    back_normed1 = times_transposed(back_proj_b, w_qkv)
    back_norm1, grad_norm1_part = norm_backward(resid_in, inv_rms1, gain1, back_normed1)
    back_tokens = back_middle + back_norm1
    grad_norm1, grad_qkv, grad_bias, grad_out, grad_norm2 = (
        lax.psum_scatter(
            grad_norm1_part.astype(jnp.bfloat16), "group", scatter_dimension=0, tiled=True
        ).astype(jnp.float32),
        lax.psum_scatter(
            grad_qkv_part.astype(jnp.bfloat16), "group", scatter_dimension=0, tiled=True
        ).astype(jnp.float32),
        lax.psum_scatter(
            grad_bias_part.astype(jnp.bfloat16), "group", scatter_dimension=0, tiled=True
        ).astype(jnp.float32),
        lax.psum_scatter(
            grad_out_part.astype(jnp.bfloat16), "group", scatter_dimension=0, tiled=True
        ).astype(jnp.float32),
        lax.psum_scatter(
            grad_norm2_part.astype(jnp.bfloat16), "group", scatter_dimension=0, tiled=True
        ).astype(jnp.float32),
    )
    grad_norm1, grad_qkv, grad_bias, grad_out, grad_norm2, grad_gate, grad_up, grad_down = (
        lax.psum(grad_norm1.astype(jnp.bfloat16), "replica").astype(jnp.float32),
        lax.psum(grad_qkv.astype(jnp.bfloat16), "replica").astype(jnp.float32),
        lax.psum(grad_bias.astype(jnp.bfloat16), "replica").astype(jnp.float32),
        lax.psum(grad_out.astype(jnp.bfloat16), "replica").astype(jnp.float32),
        lax.psum(grad_norm2.astype(jnp.bfloat16), "replica").astype(jnp.float32),
        lax.psum(grad_gate.astype(jnp.bfloat16), "replica").astype(jnp.float32),
        lax.psum(grad_up.astype(jnp.bfloat16), "replica").astype(jnp.float32),
        lax.psum(grad_down.astype(jnp.bfloat16), "replica").astype(jnp.float32),
    )
    shape_out = (sequences, length, model_width)
    return (
        result.reshape(shape_out),
        back_tokens.reshape(shape_out),
        grad_norm1,
        grad_qkv,
        grad_bias,
        grad_out,
        grad_norm2,
        grad_gate,
        grad_up,
        grad_down,
    )


def solution(mesh):
    in_specs = (
        P(("group", "replica"), None, None),
        P(("group", "replica"), None),
        P("group"),
        P("group", None),
        P("group"),
        P("group", None),
        P("group"),
        P(None, "group"),
        P(None, "group"),
        P("group", None),
        P(("group", "replica"), None, None),
    )
    out_specs = (
        P(("group", "replica"), None, None),
        P(("group", "replica"), None, None),
        P("group"),
        P("group", None),
        P("group"),
        P("group", None),
        P("group"),
        P(None, "group"),
        P(None, "group"),
        P("group", None),
    )
    return jax.shard_map(
        on_device, mesh=mesh, in_specs=in_specs, out_specs=out_specs, check_vma=False
    )
```

profile of v0, /device:TPU:0, one launch (start us, length us, event | category | flops | bytes accessed | tf_op | source)
XLA Modules:
  0.0 505.1 jit_solution(13327327023692084482)
XLA Ops:
  14.7 5.9 %all-reduce.9 = (bf16[1152]{0:T(1024)(128)(2,1)S(1)}, bf16[896]{0:T(1024)(128)(2,1)S(1)}, bf16[896]{0:T(1024)(128)(2,1)S(1)}) all-reduce(bf16[1152]{0:T(1024)(128)(2,1)S(1)} %dynamic-update-slice.1, bf16[896]{0:T(1024)(128)(2,1)S(1)} %dynamic-update-slice, ...), channel_id=1, replica_groups=mesh['group'=2,'replica'=16] {'group'}, use_global_device_ids=true, to_apply=%add.1 | all-reduce | flops 2944 | bytes 11776
  21.0 14.6 %all-gather = bf16[1,288,896]{2,1,0:T(8,128)(2,1)} all-gather(bf16[1,144,896]{2,1,0:T(8,128)(2,1)S(1)} %copy-done.6), channel_id=2, replica_groups=mesh['group'=2,'replica'=16] {'group'}, dimensions={1}, use_global_device_ids=true | all-gather | bytes 774144 | tf_op jit(solution)/shard_map/all_gather | solution.py:136
  35.6 15.0 %all-gather.4.cloned.1.call-done = bf16[896,1152]{1,0:T(8,128)(2,1)} async-done(((bf16[448,1152]{1,0:T(8,128)(2,1)}), bf16[896,1152]{1,0:T(8,128)(2,1)}) %all-gather.4.cloned.1.call-update) | async-done | bytes 2064400 | tf_op jit(solution)/shard_map/all_gather | solution.py:104
  50.6 2.2 convolution_add_fusion
  56.6 23.2 %all-gather.6.cloned.1.call-done = bf16[896,896]{1,0:T(8,128)(2,1)} async-done(((bf16[448,896]{1,0:T(8,128)(2,1)}), bf16[896,896]{1,0:T(8,128)(2,1)}) %all-gather.6.cloned.1.call-update) | async-done | bytes 1605648 | tf_op jit(solution)/shard_map/all_gather | solution.py:106
  79.8 2.0 multiply_reduce_fusion
  82.0 8.9 %all_gather.30 = bf16[288,896]{1,0:T(8,128)(2,1)S(1)} all-gather(bf16[144,896]{1,0:T(8,128)(2,1)S(1)} %multiply_convert_fusion.3), channel_id=1, replica_groups=mesh['group'=2,'replica'=16] {'group'}, dimensions={0}, use_global_device_ids=true | all-gather | bytes 774144 | tf_op jit(solution)/shard_map/all_gather | solution.py:135
  91.0 4.1 fusion.53
  95.2 1.7 fusion.52
  96.9 4.0 multiply_convert_fusion
  100.9 1.7 fusion.54
  102.7 2.5 fusion.6
  105.3 5.1 %convolution_convert_fusion.5 = bf16[288,896]{1,0:T(8,128)(2,1)} fusion(bf16[288,2432]{1,0:T(8,128)(2,1)} %get-tuple-element.30, bf16[2432,896]{1,0:T(8,128)(2,1)} %param.20), kind=kOutput, calls=%fused_computation.22 | convolution fusion | flops 1255403520 | bytes 6275072 | tf_op jit(solution)/shard_map/dot_general | solution.py:60
  110.5 9.4 %reduce-scatter.7.cloned.1.call-done = bf16[144,896]{1,0:T(8,128)(2,1)} async-done(((bf16[288,896]{1,0:T(8,128)(2,1)}), bf16[144,896]{1,0:T(8,128)(2,1)}) %reduce-scatter.7.cloned.1.call-update) | async-done | bytes 258064 | tf_op jit(solution)/shard_map/reduce_scatter | solution.py:155
  121.0 16.1 %reduce-scatter.5.cloned.1.call-done = bf16[144,896]{1,0:T(8,128)(2,1)} async-done(((bf16[288,896]{1,0:T(8,128)(2,1)}), bf16[144,896]{1,0:T(8,128)(2,1)}) %reduce-scatter.5.cloned.1.call-update) | async-done | bytes 258064 | tf_op jit(solution)/shard_map/reduce_scatter | solution.py:143
  137.1 2.2 fusion.12
  139.3 3.0 convolution_convert_fusion.4
  142.6 2.7 convolution_convert_fusion.7
  152.3 2.2 convolution_convert_fusion.3
  154.9 4.7 convolution_convert_fusion
  159.6 4.6 convolution_convert_fusion.1
  164.2 4.6 convolution_convert_fusion.2
  168.9 34.2 %reduce-scatter.9.cloned.1.call-done = bf16[448,1152]{1,0:T(8,128)(2,1)} async-done(((bf16[896,1152]{1,0:T(8,128)(2,1)}), bf16[448,1152]{1,0:T(8,128)(2,1)}) %reduce-scatter.9.cloned.1.call-update) | async-done | bytes 1032208 | tf_op jit(solution)/shard_map/reduce_scatter | solution.py:209
  204.7 1.6 fusion.25
  206.3 5.0 all-reduce.8
  211.5 33.8 %all-reduce.6 = (bf16[448]{0:T(512)(128)(2,1)S(1)}, bf16[576]{0:T(1024)(128)(2,1)S(1)}, bf16[448]{0:T(512)(128)(2,1)S(1)}) all-reduce(bf16[448]{0:T(512)(128)(2,1)S(1)} %dynamic-slice.4, bf16[576]{0:T(1024)(128)(2,1)S(1)} %dynamic-slice.6, bf16[448]{0:T(512)(128)(2,1)S(1)} %dynamic-slice.8), channel_id=1, replica_groups=mesh['group'=2,'replica'=16] {'replica'}, use_global_device_ids=true, to_apply=%region_12.13 | all-reduce | flops 1472 | bytes 5888 | tf_op jit(solution)/shard_map/psum | solution.py:223
  247.0 2.1 fusion.22
  249.1 232.0 %all-reduce.12.cloned.1.call-done = (bf16[448,1152]{1,0:T(8,128)(2,1)}, bf16[448,896]{1,0:T(8,128)(2,1)}, bf16[896,2432]{1,0:T(8,128)(2,1)}, bf16[896,2432]{1,0:T(8,128)(2,1)}, bf16[2432,896]{1,0:T(8,128)(2,1)}) async-done(((bf16[448,1152]{1,0:T(8,128)(2,1)}, bf16[448,896]{1,0:T(8,128)(2,1)}, bf16[896,2432]{1,0:T(8,128)(2,1)}, bf16[896,2432]{1,0:T(8,128)(2,1)}, bf16[2432,896]{1,0:T(8,128)(2,1)}), ...) | async-done | bytes 14909456 | tf_op jit(solution)/shard_map/psum | solution.py:224
  481.1 2.8 convert_element_type.176
  485.2 4.9 convert_element_type.184
  490.1 4.1 convert_element_type.186
  494.1 4.1 convert_element_type.188
  (172 shorter events, 22.5 us)
Async XLA Ops:
  7.2 6.1 %copy-start.2 = (bf16[1,144,896]{2,1,0:T(8,128)(2,1)S(1)}, bf16[1,144,896]{2,1,0:T(8,128)(2,1)}, u32[]{:S(2)}) copy-start(bf16[1,144,896]{2,1,0:T(8,128)(2,1)} %param.11) | copy-start | bytes 774148
  7.2 6.8 %copy-start.28 = (bf16[448]{0:T(512)(128)(2,1)S(1)}, bf16[448]{0:T(512)(128)(2,1)}, u32[]{:S(2)}) copy-start(bf16[448]{0:T(512)(128)(2,1)} %param.13) | copy-start | bytes 2692
  7.2 7.0 %copy-start.29 = (bf16[448]{0:T(512)(128)(2,1)S(1)}, bf16[448]{0:T(512)(128)(2,1)}, u32[]{:S(2)}) copy-start(bf16[448]{0:T(512)(128)(2,1)} %param.17) | copy-start | bytes 2692
  7.2 7.2 %copy-start.27 = (bf16[576]{0:T(1024)(128)(2,1)S(1)}, bf16[576]{0:T(1024)(128)(2,1)}, u32[]{:S(2)}) copy-start(bf16[576]{0:T(1024)(128)(2,1)} %param.15) | copy-start | bytes 3460
  7.2 13.8 %copy-start.6 = (bf16[1,144,896]{2,1,0:T(8,128)(2,1)S(1)}, bf16[1,144,896]{2,1,0:T(8,128)(2,1)}, u32[]{:S(2)}) copy-start(bf16[1,144,896]{2,1,0:T(8,128)(2,1)} %param.21) | copy-start | bytes 774148
  7.2 43.4 %all-gather.4.cloned.1.call-start = ((), (), s32[]{:S(2)}) async-start(), calls=%async_computation.4 | async-start | bytes 3096576 | tf_op jit(solution)/shard_map/all_gather | solution.py:104
  8.0 71.8 %all-gather.6.cloned.1.call-start = ((), (), s32[]{:S(2)}) async-start(), calls=%async_computation.5 | async-start | bytes 2408448 | tf_op jit(solution)/shard_map/all_gather | solution.py:106
  8.7 111.1 %reduce-scatter.7.cloned.1.call-start = ((), (), s32[]{:S(2)}) async-start(), calls=%async_computation.7 | async-start | bytes 774144 | tf_op jit(solution)/shard_map/reduce_scatter | solution.py:155
  20.8 34.3 %copy-start.16 = (f32[144,32]{0,1:T(8,128)}, f32[144,32]{0,1:T(8,128)S(1)}, u32[]{:S(2)}) copy-start(f32[144,32]{0,1:T(8,128)S(1)} %get-tuple-element.44) | copy-start | bytes 55300
  20.9 32.6 %copy-start.12 = (f32[144,32]{1,0:T(8,128)}, f32[144,32]{1,0:T(8,128)S(1)}, u32[]{:S(2)}) copy-start(f32[144,32]{1,0:T(8,128)S(1)} %copy.77) | copy-start | bytes 55300
  21.0 32.5 %copy-start.14 = (f32[144,32]{1,0:T(8,128)}, f32[144,32]{1,0:T(8,128)S(1)}, u32[]{:S(2)}) copy-start(f32[144,32]{1,0:T(8,128)S(1)} %copy.78) | copy-start | bytes 55300
  56.5 34.4 %copy-start.4 = (bf16[2,64,7,144]{3,1,2,0:T(8,128)(2,1)}, bf16[2,64,7,144]{3,1,2,0:T(8,128)(2,1)S(1)}, u32[]{:S(2)}) copy-start(bf16[2,64,7,144]{3,1,2,0:T(8,128)(2,1)S(1)} %convolution_convert_fusion.6) | copy-start | bytes 774148
  82.0 13.1 %slice-start.4 = ((s8[4358144]{0:T(1024)(128)(4,1)}), s8[4194304]{0:T(1024)(128)(4,1)S(1)}, s32[]{:S(2)}) async-start(s8[4358144]{0:T(1024)(128)(4,1)} %bitcast.142), calls=%async_computation.15 | async-start | bytes 8388608
  90.9 4.2 copy-start.20
  90.9 4.2 slice-start.5
  91.0 5.9 %slice-start.8 = ((s8[4358144]{0:T(1024)(128)(4,1)}), s8[4194304]{0:T(1024)(128)(4,1)S(1)}, s32[]{:S(2)}) async-start(s8[4358144]{0:T(1024)(128)(4,1)} %bitcast.146), calls=%async_computation.19 | async-start | bytes 8388608
  95.2 7.5 %slice-start.6 = ((s8[4358144]{0:T(1024)(128)(4,1)}), s8[4194304]{0:T(1024)(128)(4,1)S(1)}, s32[]{:S(2)}) async-start(s8[4358144]{0:T(1024)(128)(4,1)} %bitcast.144), calls=%async_computation.17 | async-start | bytes 8388608
  96.9 5.8 %slice-start.7 = ((s8[4358144]{0:T(1024)(128)(4,1)}), s8[163840]{0:T(1024)(128)(4,1)S(1)}, s32[]{:S(2)}) async-start(s8[4358144]{0:T(1024)(128)(4,1)} %bitcast.144), calls=%async_computation.18 | async-start | bytes 327680
  105.2 31.9 %reduce-scatter.5.cloned.1.call-start = ((), (), s32[]{:S(2)}) async-start(), calls=%async_computation.6 | async-start | bytes 774144 | tf_op jit(solution)/shard_map/reduce_scatter | solution.py:143
  110.4 58.5 %reduce-scatter.11.cloned.1.call-start = ((), (), s32[]{:S(2)}) async-start(), calls=%async_computation.9 | async-start | bytes 2408448 | tf_op jit(solution)/shard_map/reduce_scatter | solution.py:215
  142.3 60.8 %reduce-scatter.9.cloned.1.call-start = ((), (), s32[]{:S(2)}) async-start(), calls=%async_computation.8 | async-start | bytes 3096576 | tf_op jit(solution)/shard_map/reduce_scatter | solution.py:209
  154.6 5.1 %copy-start.21 = (bf16[288,896]{1,0:T(8,128)(2,1)S(1)}, bf16[288,896]{1,0:T(8,128)(2,1)}, u32[]{:S(2)}) copy-start(bf16[288,896]{1,0:T(8,128)(2,1)} %copy-done.20) | copy-start | bytes 1548292
  154.6 326.5 %all-reduce.12.cloned.1.call-start = ((), (), s32[]{:S(2)}) async-start(), calls=%async_computation.10 | async-start | bytes 29818880 | tf_op jit(solution)/shard_map/psum | solution.py:224
  154.9 4.7 copy-start.34
  159.6 4.6 copy-start.32
  204.6 42.4 %copy-start.1 = (f32[144,896]{1,0:T(8,128)S(1)}, f32[144,896]{1,0:T(8,128)}, u32[]{:S(2)}) copy-start(f32[144,896]{1,0:T(8,128)} %copy-done) | copy-start | bytes 1548292
  204.6 42.4 %copy-start.26 = (f32[144]{0:T(256)S(1)}, f32[144]{0:T(256)}, u32[]{:S(2)}) copy-start(f32[144]{0:T(256)} %get-tuple-element.45) | copy-start | bytes 1732
  481.1 4.1 copy-start.3
  483.9 6.1 %slice-start.2 = ((s8[4358144]{0:T(1024)(128)(4,1)}), s8[4194304]{0:T(1024)(128)(4,1)S(1)}, s32[]{:S(2)}) async-start(s8[4358144]{0:T(1024)(128)(4,1)} %bitcast.125), calls=%async_computation.13 | async-start | bytes 8388608
  485.2 4.9 slice-start.3
  485.2 9.0 %slice-start = ((s8[4358144]{0:T(1024)(128)(4,1)}), s8[4194304]{0:T(1024)(128)(4,1)S(1)}, s32[]{:S(2)}) async-start(s8[4358144]{0:T(1024)(128)(4,1)} %bitcast.123), calls=%async_computation.11 | async-start | bytes 8388608
  490.1 4.1 slice-start.1
  (20 other events, 31.8 us)
Sparse Core Ops, SparseCore 0:
  9.6 40.9 all-gather.3
  52.2 27.5 all-gather.5
  105.3 14.4 reduce-scatter.6
  122.6 14.4 reduce-scatter.4
  142.4 26.4 reduce-scatter.10
  171.6 31.4 reduce-scatter.8
  209.3 271.7 all-reduce.11
where the time goes:
time: 506 us; the launch traced here: 505 us
  waiting for transfers between devices  332 us (66%)
  blocking collectives  68.2 us (13%)
  matrix products  49.6 us (10%)
  other arithmetic  29.5 us (6%)
  between operations  17.6 us (3%)
  local copies, waits for them, and re-layouts  7.93 us (2%)
    psum x1, waiting for transfers between devices, on_device(): lax.psum(grad_qkv.astype(jnp.bfloat16), 'replica').astype(jnp.float32)  232 us
    reduce_scatter x1, waiting for transfers between devices, on_device(): lax.psum_scatter(grad_qkv_part.astype(jnp.bfloat16), 'group', scatter_dim...  34.2 us
    psum x1, blocking collectives, on_device(): lax.psum(grad_norm1.astype(jnp.bfloat16), 'replica').astype(jnp.float32)  33.8 us
    all_gather x1, waiting for transfers between devices, on_device(): lax.all_gather(out_weight, 'group', axis=0, tiled=True)  23.2 us
    dot_general x5, matrix products, outer_sum(): lax.dot_general(left, right, (((0,), (0,)), ((), ())), preferred_element_...  19.1 us
    reduce_scatter x1, waiting for transfers between devices, on_device(): lax.psum_scatter(matmul(activ_b, down_weight).astype(jnp.bfloat16), 'grou...  16.1 us
    dot_general x5, matrix products, matmul(): return jnp.dot(left, right, preferred_element_type=jnp.float32)  15.2 us
    all_gather x1, waiting for transfers between devices, on_device(): lax.all_gather(qkv_weight, 'group', axis=0, tiled=True)  15 us
  transfers between devices with their start and end apart: 7, of which 7 were waited for; matrix products, arithmetic and copies ran while one was open for 9% of the time, Pallas kernels for 0%

commit v1 on v0

--- a/solution.py
+++ b/solution.py
@@ -9,6 +9,10 @@
 EPSILON = 1e-06
 ROPE_BASE = 1000000.0
 NEG_LARGE = -1e30
+
+
+def tell_the_members_all(frame_in, axis_key):
+    return lax.all_gather(frame_in, axis_key).sum(axis=0)
 
 
 def doc_layout(segments, head_dim):
@@ -221,7 +225,7 @@
     )
     grad_norm1, grad_qkv, grad_bias, grad_out, grad_norm2, grad_gate, grad_up, grad_down = (
         lax.psum(grad_norm1.astype(jnp.bfloat16), "replica").astype(jnp.float32),
-        lax.psum(grad_qkv.astype(jnp.bfloat16), "replica").astype(jnp.float32),
+        tell_the_members_all(grad_qkv.astype(jnp.bfloat16), "replica").astype(jnp.float32),
         lax.psum(grad_bias.astype(jnp.bfloat16), "replica").astype(jnp.float32),
         lax.psum(grad_out.astype(jnp.bfloat16), "replica").astype(jnp.float32),
         lax.psum(grad_norm2.astype(jnp.bfloat16), "replica").astype(jnp.float32),

time: 506 us -> 610 us (1.21)
  waiting for transfers between devices: 332 us -> 426 us
  other arithmetic: 29.5 us -> 39.7 us
    all_gather x0 -> x1, waiting for transfers between devices: none -> 110 us  [tell_the_members_all(): return lax.all_gather(frame_in, axis_key).sum(axis=0)]
    psum x1, waiting for transfers between devices: 232 us -> 216 us  [on_device(): lax.psum(grad_out.astype(jnp.bfloat16), 'replica').astype(jnp.float32)]
    reduce_sum x0 -> x1, other arithmetic: none -> 8.84 us  [tell_the_members_all(): return lax.all_gather(frame_in, axis_key).sum(axis=0)]
  transfers between devices with their start and end apart: 7 -> 8, of which waited for: 7 -> 8; matrix products, arithmetic and copies ran while one was open for 9% -> 11% of each run, Pallas kernels for 0% -> 0%
where the time goes in v1:
time: 610 us; the launch traced here: 609 us
  waiting for transfers between devices  426 us (70%)
  blocking collectives  68.2 us (11%)
  matrix products  49.6 us (8%)
  other arithmetic  39.7 us (7%)
  between operations  17.5 us (3%)
  local copies, waits for them, and re-layouts  7.88 us (1%)
    psum x1, waiting for transfers between devices, on_device(): lax.psum(grad_out.astype(jnp.bfloat16), 'replica').astype(jnp.float32)  216 us
    all_gather x1, waiting for transfers between devices, tell_the_members_all(): return lax.all_gather(frame_in, axis_key).sum(axis=0)  110 us
    reduce_scatter x1, waiting for transfers between devices, on_device(): lax.psum_scatter(grad_qkv_part.astype(jnp.bfloat16), 'group', scatter_dim...  34.1 us
    psum x1, blocking collectives, on_device(): lax.psum(grad_norm1.astype(jnp.bfloat16), 'replica').astype(jnp.float32)  33.8 us
    all_gather x1, waiting for transfers between devices, on_device(): lax.all_gather(out_weight, 'group', axis=0, tiled=True)  23.2 us
    dot_general x5, matrix products, outer_sum(): lax.dot_general(left, right, (((0,), (0,)), ((), ())), preferred_element_...  19.1 us
    reduce_scatter x1, waiting for transfers between devices, on_device(): lax.psum_scatter(matmul(activ_b, down_weight).astype(jnp.bfloat16), 'grou...  16.1 us
    dot_general x5, matrix products, matmul(): return jnp.dot(left, right, preferred_element_type=jnp.float32)  15.2 us
  transfers between devices with their start and end apart: 8, of which 8 were waited for; matrix products, arithmetic and copies ran while one was open for 11% of the time, Pallas kernels for 0%

profile of v1, /device:TPU:0, one launch (start us, length us, event | category | flops | bytes accessed | tf_op | source)
XLA Modules:
  0.0 609.2 jit_solution(2737720889557035145)
XLA Ops:
  14.6 5.9 all-reduce.9
  21.0 14.6 %all-gather = bf16[1,288,896]{2,1,0:T(8,128)(2,1)} all-gather(bf16[1,144,896]{2,1,0:T(8,128)(2,1)S(1)} %copy-done.5), channel_id=2, replica_groups=mesh['group'=2,'replica'=16] {'group'}, dimensions={1}, use_global_device_ids=true | all-gather | bytes 774144 | tf_op jit(solution)/shard_map/all_gather | solution.py:140
  35.6 15.0 %all-gather.6.cloned.1.call-done = bf16[896,1152]{1,0:T(8,128)(2,1)} async-done(((bf16[448,1152]{1,0:T(8,128)(2,1)}), bf16[896,1152]{1,0:T(8,128)(2,1)}) %all-gather.6.cloned.1.call-update) | async-done | bytes 2064400 | tf_op jit(solution)/shard_map/all_gather | solution.py:108
  50.6 2.2 convolution_add_fusion
  56.6 23.2 %all-gather.8.cloned.1.call-done = bf16[896,896]{1,0:T(8,128)(2,1)} async-done(((bf16[448,896]{1,0:T(8,128)(2,1)}), bf16[896,896]{1,0:T(8,128)(2,1)}) %all-gather.8.cloned.1.call-update) | async-done | bytes 1605648 | tf_op jit(solution)/shard_map/all_gather | solution.py:110
  79.8 2.0 multiply_reduce_fusion
  82.0 8.9 %all_gather.36 = bf16[288,896]{1,0:T(8,128)(2,1)S(1)} all-gather(bf16[144,896]{1,0:T(8,128)(2,1)S(1)} %multiply_convert_fusion.3), channel_id=1, replica_groups=mesh['group'=2,'replica'=16] {'group'}, dimensions={0}, use_global_device_ids=true | all-gather | bytes 774144 | tf_op jit(solution)/shard_map/all_gather | solution.py:139
  90.9 4.1 fusion.53
  96.9 4.0 multiply_convert_fusion
  100.9 1.7 fusion.54
  102.7 2.5 fusion.6
  105.3 5.1 convolution_convert_fusion.5
  110.4 9.4 %reduce-scatter.7.cloned.1.call-done = bf16[144,896]{1,0:T(8,128)(2,1)} async-done(((bf16[288,896]{1,0:T(8,128)(2,1)}), bf16[144,896]{1,0:T(8,128)(2,1)}) %reduce-scatter.7.cloned.1.call-update) | async-done | bytes 258064 | tf_op jit(solution)/shard_map/reduce_scatter | solution.py:159
  121.0 16.1 %reduce-scatter.5.cloned.1.call-done = bf16[144,896]{1,0:T(8,128)(2,1)} async-done(((bf16[288,896]{1,0:T(8,128)(2,1)}), bf16[144,896]{1,0:T(8,128)(2,1)}) %reduce-scatter.5.cloned.1.call-update) | async-done | bytes 258064 | tf_op jit(solution)/shard_map/reduce_scatter | solution.py:147
  137.1 2.2 fusion.12
  139.3 3.0 convolution_convert_fusion.4
  142.6 2.7 convolution_convert_fusion.7
  152.3 2.2 convolution_convert_fusion.3
  154.6 4.7 convolution_convert_fusion
  159.3 4.6 convolution_convert_fusion.1
  163.9 4.6 convolution_convert_fusion.2
  169.0 34.1 %reduce-scatter.9.cloned.1.call-done = bf16[448,1152]{1,0:T(8,128)(2,1)} async-done(((bf16[896,1152]{1,0:T(8,128)(2,1)}), bf16[448,1152]{1,0:T(8,128)(2,1)}) %reduce-scatter.9.cloned.1.call-update) | async-done | bytes 1032208 | tf_op jit(solution)/shard_map/reduce_scatter | solution.py:213
  206.1 5.0 all-reduce.8
  211.3 33.8 %all-reduce.6 = (bf16[448]{0:T(512)(128)(2,1)S(1)}, bf16[576]{0:T(1024)(128)(2,1)S(1)}, bf16[448]{0:T(512)(128)(2,1)S(1)}) all-reduce(bf16[448]{0:T(512)(128)(2,1)S(1)} %dynamic-slice.4, bf16[576]{0:T(1024)(128)(2,1)S(1)} %dynamic-slice.6, bf16[448]{0:T(512)(128)(2,1)S(1)} %dynamic-slice.8), channel_id=1, replica_groups=mesh['group'=2,'replica'=16] {'replica'}, use_global_device_ids=true, to_apply=%region_12.13 | all-reduce | flops 1472 | bytes 5888 | tf_op jit(solution)/shard_map/psum | solution.py:227
  246.8 2.0 fusion.22
  248.9 216.0 %all-reduce.12.cloned.1.call-done = (bf16[448,896]{1,0:T(8,128)(2,1)}, bf16[896,2432]{1,0:T(8,128)(2,1)}, bf16[896,2432]{1,0:T(8,128)(2,1)}, bf16[2432,896]{1,0:T(8,128)(2,1)}) async-done(((bf16[448,896]{1,0:T(8,128)(2,1)}, bf16[896,2432]{1,0:T(8,128)(2,1)}, bf16[896,2432]{1,0:T(8,128)(2,1)}, bf16[2432,896]{1,0:T(8,128)(2,1)}), (bf16[448,896]{1,0:T(8,128)(2,1)}, bf16[896,2432]{1,0:T(8,128)(2,1)}, ...) | async-done | bytes 13877264 | tf_op jit(solution)/shard_map/psum | solution.py:230
  464.8 2.5 convert_element_type.182
  467.4 6.4 %convert_element_type.186 = f32[896,2432]{1,0:T(8,128)} convert(bf16[896,2432]{1,0:T(8,128)(2,1)} %get-tuple-element.18) | non-fusion elementwise | flops 2179072 | bytes 13074432 | tf_op jit(solution)/shard_map/convert_element_type | solution.py:232
  473.8 4.1 convert_element_type.188
  477.9 4.1 convert_element_type.190
  482.0 110.1 %all-gather.10.cloned.1.call-done = bf16[7168,1152]{1,0:T(8,128)(2,1)} async-done(((bf16[448,1152]{1,0:T(8,128)(2,1)}), bf16[7168,1152]{1,0:T(8,128)(2,1)}) %all-gather.10.cloned.1.call-update) | async-done | bytes 16515088 | tf_op jit(solution)/shard_map/all_gather | solution.py:15
  592.0 8.8 %reduce_sum.110 = bf16[448,1152]{1,0:T(8,128)(2,1)S(1)} reduce(bf16[16,448,1152]{2,1,0:T(8,128)(2,1)} %bitcast.124, bf16[]{:T(256)} %constant.32.clone.1), dimensions={0}, to_apply=%region_14.15 | reduce | flops 7741440 | bytes 17547266 | tf_op jit(solution)/shard_map/reduce_sum | solution.py:15
  (172 shorter events, 25.9 us)
Async XLA Ops:
  7.2 6.1 copy-start.2
  7.2 6.7 %copy-start.26 = (bf16[448]{0:T(512)(128)(2,1)S(1)}, bf16[448]{0:T(512)(128)(2,1)}, u32[]{:S(2)}) copy-start(bf16[448]{0:T(512)(128)(2,1)} %param.13) | copy-start | bytes 2692
  7.2 6.9 %copy-start.27 = (bf16[448]{0:T(512)(128)(2,1)S(1)}, bf16[448]{0:T(512)(128)(2,1)}, u32[]{:S(2)}) copy-start(bf16[448]{0:T(512)(128)(2,1)} %param.17) | copy-start | bytes 2692
  7.2 7.2 %copy-start.25 = (bf16[576]{0:T(1024)(128)(2,1)S(1)}, bf16[576]{0:T(1024)(128)(2,1)}, u32[]{:S(2)}) copy-start(bf16[576]{0:T(1024)(128)(2,1)} %param.15) | copy-start | bytes 3460
  7.2 13.7 %copy-start.5 = (bf16[1,144,896]{2,1,0:T(8,128)(2,1)S(1)}, bf16[1,144,896]{2,1,0:T(8,128)(2,1)}, u32[]{:S(2)}) copy-start(bf16[1,144,896]{2,1,0:T(8,128)(2,1)} %param.21) | copy-start | bytes 774148
  7.2 43.4 %all-gather.6.cloned.1.call-start = ((), (), s32[]{:S(2)}) async-start(), calls=%async_computation.4 | async-start | bytes 3096576 | tf_op jit(solution)/shard_map/all_gather | solution.py:108
  8.0 71.8 %all-gather.8.cloned.1.call-start = ((), (), s32[]{:S(2)}) async-start(), calls=%async_computation.5 | async-start | bytes 2408448 | tf_op jit(solution)/shard_map/all_gather | solution.py:110
  8.7 111.1 %reduce-scatter.7.cloned.1.call-start = ((), (), s32[]{:S(2)}) async-start(), calls=%async_computation.7 | async-start | bytes 774144 | tf_op jit(solution)/shard_map/reduce_scatter | solution.py:159
  20.7 34.3 %copy-start.14 = (f32[144,32]{0,1:T(8,128)}, f32[144,32]{0,1:T(8,128)S(1)}, u32[]{:S(2)}) copy-start(f32[144,32]{0,1:T(8,128)S(1)} %get-tuple-element.43) | copy-start | bytes 55300
  20.9 32.7 %copy-start.10 = (f32[144,32]{1,0:T(8,128)}, f32[144,32]{1,0:T(8,128)S(1)}, u32[]{:S(2)}) copy-start(f32[144,32]{1,0:T(8,128)S(1)} %copy.77) | copy-start | bytes 55300
  21.0 32.6 %copy-start.12 = (f32[144,32]{1,0:T(8,128)}, f32[144,32]{1,0:T(8,128)S(1)}, u32[]{:S(2)}) copy-start(f32[144,32]{1,0:T(8,128)S(1)} %copy.78) | copy-start | bytes 55300
  56.5 34.4 %copy-start.3 = (bf16[2,64,7,144]{3,1,2,0:T(8,128)(2,1)}, bf16[2,64,7,144]{3,1,2,0:T(8,128)(2,1)S(1)}, u32[]{:S(2)}) copy-start(bf16[2,64,7,144]{3,1,2,0:T(8,128)(2,1)S(1)} %convolution_convert_fusion.6) | copy-start | bytes 774148
  82.0 13.1 %slice-start.4 = ((s8[4358144]{0:T(1024)(128)(4,1)}), s8[4194304]{0:T(1024)(128)(4,1)S(1)}, s32[]{:S(2)}) async-start(s8[4358144]{0:T(1024)(128)(4,1)} %bitcast.144), calls=%async_computation.16 | async-start | bytes 8388608
  90.9 4.2 copy-start.18
  90.9 4.2 slice-start.5
  90.9 5.9 slice-start.8
  95.2 7.5 %slice-start.6 = ((s8[4358144]{0:T(1024)(128)(4,1)}), s8[4194304]{0:T(1024)(128)(4,1)S(1)}, s32[]{:S(2)}) async-start(s8[4358144]{0:T(1024)(128)(4,1)} %bitcast.146), calls=%async_computation.18 | async-start | bytes 8388608
  96.9 5.8 slice-start.7
  105.2 31.9 %reduce-scatter.5.cloned.1.call-start = ((), (), s32[]{:S(2)}) async-start(), calls=%async_computation.6 | async-start | bytes 774144 | tf_op jit(solution)/shard_map/reduce_scatter | solution.py:147
  110.4 58.5 %reduce-scatter.11.cloned.1.call-start = ((), (), s32[]{:S(2)}) async-start(), calls=%async_computation.9 | async-start | bytes 2408448 | tf_op jit(solution)/shard_map/reduce_scatter | solution.py:219
  142.3 60.8 %reduce-scatter.9.cloned.1.call-start = ((), (), s32[]{:S(2)}) async-start(), calls=%async_computation.8 | async-start | bytes 3096576 | tf_op jit(solution)/shard_map/reduce_scatter | solution.py:213
  154.5 4.8 copy-start.19
  154.6 310.3 %all-reduce.12.cloned.1.call-start = ((), (), s32[]{:S(2)}) async-start(), calls=%async_computation.11 | async-start | bytes 27754496 | tf_op jit(solution)/shard_map/psum | solution.py:230
  154.6 4.7 copy-start.32
  159.3 4.6 copy-start.30
  168.9 35.6 %copy-start.4 = (bf16[896,1152]{1,0:T(8,128)(2,1)S(1)}, bf16[896,1152]{1,0:T(8,128)(2,1)}, u32[]{:S(2)}) copy-start(bf16[896,1152]{1,0:T(8,128)(2,1)} %all-gather.6.cloned.1.call-done) | copy-start | bytes 6193156
  169.0 423.1 %all-gather.10.cloned.1.call-start = ((), (), s32[]{:S(2)}) async-start(), calls=%async_computation.10 | async-start | bytes 17547264 | tf_op jit(solution)/shard_map/all_gather | solution.py:15
  204.4 42.4 %copy-start.1 = (f32[144,896]{1,0:T(8,128)S(1)}, f32[144,896]{1,0:T(8,128)}, u32[]{:S(2)}) copy-start(f32[144,896]{1,0:T(8,128)} %copy-done) | copy-start | bytes 1548292
  204.4 42.4 %copy-start.24 = (f32[144]{0:T(256)S(1)}, f32[144]{0:T(256)}, u32[]{:S(2)}) copy-start(f32[144]{0:T(256)} %get-tuple-element.44) | copy-start | bytes 1732
  464.8 9.0 %slice-start.2 = ((s8[4358144]{0:T(1024)(128)(4,1)}), s8[4194304]{0:T(1024)(128)(4,1)S(1)}, s32[]{:S(2)}) async-start(s8[4358144]{0:T(1024)(128)(4,1)} %bitcast.127), calls=%async_computation.14 | async-start | bytes 8388608
  467.4 6.5 %slice-start.3 = ((s8[4358144]{0:T(1024)(128)(4,1)}), s8[163840]{0:T(1024)(128)(4,1)S(1)}, s32[]{:S(2)}) async-start(s8[4358144]{0:T(1024)(128)(4,1)} %bitcast.127), calls=%async_computation.15 | async-start | bytes 327680
  467.4 10.5 %slice-start = ((s8[4358144]{0:T(1024)(128)(4,1)}), s8[4194304]{0:T(1024)(128)(4,1)S(1)}, s32[]{:S(2)}) async-start(s8[4358144]{0:T(1024)(128)(4,1)} %bitcast.125), calls=%async_computation.12 | async-start | bytes 8388608
  (19 other events, 31.0 us)
Sparse Core Ops, SparseCore 0:
  9.6 40.9 all-gather.5
  52.2 27.5 all-gather.7
  105.3 14.4 reduce-scatter.6
  122.6 14.4 reduce-scatter.4
  142.4 26.4 reduce-scatter.10
  171.6 31.4 reduce-scatter.8
  208.9 255.8 all-reduce.11
  467.1 124.8 all-gather.9
